TPU v7x, 256 devices: a whole 4x4x8 slice. The times are simulated.
256 devices in a mesh: prow: 32 (over x, z), pcol: 8 (over y, core).
Axes of the slice: x: 4, y: 4, z: 8, core: 2. Of those that a mesh axis runs over, the one named last changes fastest.
Arguments:
- anc_inverse: bfloat16 [4, 32, 256, 16, 8, 256], P(None, 'prow', None, None, 'pcol'), may hold values from -6 to 6
- first_lower: bfloat16 [4, 32, 256, 256], P(None, 'prow', 'pcol'), may hold values from -0.046875 to 0.046875
- second_lower: bfloat16 [4, 32, 256, 256], P(None, 'prow', 'pcol'), may hold values from -0.0546875 to 0.0546875
- second_top: bfloat16 [256, 256], replicated, may hold values from -0.3125 to 0.3125
- struct_first: int32 [128], replicated, may hold values from 0 to 1
- struct_keep: int32 [128], replicated, may hold values from 0 to 1
- pivot_h: float32 [2, 256, 256], replicated, as said below
- pivot_s: float32 [2, 256, 256], replicated, as said below
- shifts: float32 [40], replicated, may hold values from 0.5 to 4
- pole_index: int32 [40], replicated, may hold values from 0 to 39, each once
Outputs:
- first_column: bfloat16 [4, 32, 256, 256], P(None, 'prow', 'pcol')
- first_diag: float32 [256, 256], replicated
- link_column: bfloat16 [256, 256], replicated
- second_column: bfloat16 [4, 32, 256, 256], P(None, 'prow', 'pcol')
- second_diag: float32 [256, 256], replicated
Inputs may be any that keep to these rules, and one draw needn't show every extreme that they name: `struct_first`: 1 marks a block row of the first supernode's structure. `struct_keep`: 1 marks a structure block that the second supernode keeps. `pole_index`: each pole appears once. `pivot_h`: symmetric, with a positive diagonal larger than each row's off-diagonal magnitudes together. `pivot_s`: symmetric, with a positive diagonal larger than each row's off-diagonal magnitudes together.
All inputs are finite; a program needn't handle non-finite values.
Results may differ from a plain program's by a relative error of at most 0.0041.
The roundings to bfloat16 on the way count: a program that leaves them out, or rounds other values in their place, can miss the bound.
Values may be sent and summed in bfloat16 or wider, within the bound.
A program may use at most 64 MiB of HBM per device.

v0:
```python
import jax
import jax.numpy as jnp
from jax import lax
from jax.sharding import PartitionSpec as P


def pivot_inverse(h_block, s_block, shift):
    factor = jnp.linalg.cholesky(h_block + shift * s_block)
    identity = jnp.eye(h_block.shape[0], dtype=jnp.float32)
    return jax.scipy.linalg.cho_solve((factor, True), identity)


def local_mask(flags, row_blocks, grid_rows, my_row):
    table = flags.reshape(row_blocks, grid_rows).astype(jnp.float32)
    return lax.dynamic_index_in_dim(table, my_row, axis=1, keepdims=False)


def per_device(
    anc_inverse,
    first_lower,
    second_lower,
    second_top,
    struct_first,
    struct_keep,
    pivot_h,
    pivot_s,
    shifts,
    pole_index,
):
    grid_rows = lax.axis_size("prow")
    grid_cols = lax.axis_size("pcol")
    my_row = lax.axis_index("prow")
    my_col = lax.axis_index("pcol")
    row_blocks = first_lower.shape[0]
    slab = first_lower.shape[2]
    width = first_lower.shape[3]
    col_blocks = anc_inverse.shape[3]
    first_mask = local_mask(struct_first, row_blocks, grid_rows, my_row)
    second_mask = first_mask * local_mask(struct_keep, row_blocks, grid_rows, my_row)
    lower_first = first_lower[:, 0] * first_mask.astype(jnp.bfloat16)[:, None, None]
    lower_second = second_lower[:, 0] * second_mask.astype(jnp.bfloat16)[:, None, None]
    stacked = jnp.concatenate([lower_first, lower_second], axis=2)[:, None]
    gathered = lax.all_gather(stacked, "prow", axis=1, tiled=True)
    grouped = gathered.reshape(row_blocks, grid_rows // grid_cols, grid_cols, slab, 2 * width)
    columns = lax.all_to_all(grouped, "pcol", split_axis=2, concat_axis=3, tiled=True)
    column_blocks = columns.reshape(col_blocks, width, 2 * width)
    inverse_rows = anc_inverse.reshape(row_blocks, width, col_blocks, width)
    totals = lax.psum(
        jnp.einsum(
            "axcy,cyz->xaz", inverse_rows, column_blocks, preferred_element_type=jnp.float32
        ),
        "pcol",
    )
    row_part = lax.dynamic_slice_in_dim(totals, my_col * slab, slab, 0)
    first_col = (-row_part[:, :, :width] * first_mask[None, :, None]).astype(jnp.bfloat16)
    bridge = jnp.einsum("raw,wz->raz", first_col, second_top, preferred_element_type=jnp.float32)
    second_col = (-(row_part[:, :, width:] + bridge) * second_mask[None, :, None]).astype(
        jnp.bfloat16
    )
    first_rows = lower_first.transpose(1, 0, 2)
    second_rows = lower_second.transpose(1, 0, 2)
    first_term = jnp.einsum(
        "ray,raz->yz", first_rows, first_col, preferred_element_type=jnp.float32
    )
    cross_term = jnp.einsum(
        "ray,raz->yz", first_col, second_rows, preferred_element_type=jnp.float32
    )
    second_term = jnp.einsum(
        "ray,raz->yz", second_rows, second_col, preferred_element_type=jnp.float32
    )
    first_sum, cross_sum, second_sum = lax.psum(
        (first_term, cross_term, second_term), ("prow", "pcol")
    )
    poles = jnp.arange(shifts.shape[0], dtype=jnp.int32)
    shift = jnp.sum(jnp.where(poles == pole_index[0], shifts, 0.0))
    first_diag = pivot_inverse(pivot_h[0], pivot_s[0], shift) - first_sum
    link_col = (
        -(
            cross_sum
            + jnp.dot(
                first_diag.astype(jnp.bfloat16), second_top, preferred_element_type=jnp.float32
            )
        )
    ).astype(jnp.bfloat16)
    second_diag = (
        pivot_inverse(pivot_h[1], pivot_s[1], shift)
        - second_sum
        - jnp.einsum("yz,yw->zw", second_top, link_col, preferred_element_type=jnp.float32)
    )
    return (
        first_col.transpose(1, 0, 2)[:, None],
        first_diag,
        link_col,
        second_col.transpose(1, 0, 2)[:, None],
        second_diag,
    )


def solution(mesh):
    return jax.shard_map(
        per_device,
        mesh=mesh,
        in_specs=(
            P(None, "prow", None, None, "pcol", None),
            P(None, "prow", "pcol", None),
            P(None, "prow", "pcol", None),
            P(),
            P(),
            P(),
            P(),
            P(),
            P(),
            P(),
        ),
        out_specs=(P(None, "prow", "pcol", None), P(), P(), P(None, "prow", "pcol", None), P()),
        check_vma=False,
    )
```

profile of v0, /device:TPU:1, one launch (start us, length us, event | category | flops | bytes accessed | tf_op | source)
XLA Modules:
  0.0 543.7 jit_solution(14048645056738182097)
XLA Ops:
  9.0 0.9 bitcast_multiply_fusion
  11.5 1.1 fusion.48
  12.7 1.1 fusion.47
  13.9 1.9 fusion.43
  18.5 11.7 %cholesky.130 = f32[128,128]{1,0:T(8,128)S(1)} custom-call(f32[128,128]{1,0:T(8,128)S(1)} %cholesky.194), custom_call_target="Cholesky" | custom-call | tf_op jit(solution)/shard_map/jit(cholesky)/cholesky | solution.py:8
  30.3 9.8 %custom-call.15 = f32[1,128,128]{1,2,0:T(8,128)S(1)} custom-call(f32[1,128,128]{2,1,0:T(8,128)S(1)} %get-tuple-element.84), custom_call_target="InvertDiagBlocksLowerTriangular" | custom-call | tf_op jit(solution)/shard_map/jit(cholesky)/cholesky | solution.py:8
  40.6 11.7 %cholesky.147 = f32[128,128]{1,0:T(8,128)S(1)} custom-call(f32[128,128]{1,0:T(8,128)S(1)} %convolution_subtract_fusion.5), custom_call_target="Cholesky" | custom-call | tf_op jit(solution)/shard_map/jit(cholesky)/cholesky | solution.py:8
  55.0 39.8 %all-gather.3.cloned.1.call-done = bf16[4,1024,512]{2,1,0:T(8,128)(2,1)} async-done(((bf16[4,32,512]{2,1,0:T(8,128)(2,1)}), bf16[4,1024,512]{2,1,0:T(8,128)(2,1)}) %all-gather.3.cloned.1.call-update) | async-done | bytes 4194320 | tf_op jit(solution)/shard_map/all_gather | solution.py:43
  94.8 4.7 copy.82
  99.5 7.9 %all-to-all-start = ((bf16[4,4,8,32,512]{4,3,1,0,2:T(8,128)(2,1)}), bf16[4,4,8,32,512]{4,3,1,0,2:T(8,128)(2,1)}, u32[]{:S(2)}, u32[]{:S(2)}) async-start(bf16[4,4,8,32,512]{4,3,1,0,2:T(8,128)(2,1)} %copy.82), calls=%async_computation | async-start | bytes 8388608 | tf_op jit(solution)/shard_map/all_to_all | solution.py:45
  107.5 4.0 while.4
  108.1 1.4 bitcast_dynamic-update-slice_fusion.4
  110.1 1.4 bitcast_dynamic-update-slice_fusion.4
  111.5 19.7 %custom-call.16 = f32[2,128,128]{1,2,0:T(8,128)S(1)} custom-call(f32[2,128,128]{2,1,0:T(8,128)S(1)} %get-tuple-element.21), custom_call_target="InvertDiagBlocksLowerTriangular" | custom-call | tf_op jit(solution)/shard_map/jit(_cho_solve)/triangular_solve | solution.py:10
  131.2 11.7 %cholesky.164 = f32[128,128]{1,0:T(8,128)S(1)} custom-call(f32[128,128]{1,0:T(8,128)S(1)} %cholesky.197), custom_call_target="Cholesky" | custom-call | tf_op jit(solution)/shard_map/jit(cholesky)/cholesky | solution.py:8
  143.0 9.8 %custom-call.17 = f32[1,128,128]{1,2,0:T(8,128)S(1)} custom-call(f32[1,128,128]{2,1,0:T(8,128)S(1)} %get-tuple-element.80), custom_call_target="InvertDiagBlocksLowerTriangular" | custom-call | tf_op jit(solution)/shard_map/jit(cholesky)/cholesky | solution.py:8
  153.3 11.7 %cholesky.181 = f32[128,128]{1,0:T(8,128)S(1)} custom-call(f32[128,128]{1,0:T(8,128)S(1)} %convolution_subtract_fusion.4), custom_call_target="Cholesky" | custom-call | tf_op jit(solution)/shard_map/jit(cholesky)/cholesky | solution.py:8
  167.6 4.0 while.5
  168.3 1.4 bitcast_dynamic-update-slice_fusion.5
  170.3 1.4 bitcast_dynamic-update-slice_fusion.5
  171.7 19.9 %custom-call.18 = f32[2,128,128]{1,2,0:T(8,128)S(1)} custom-call(f32[2,128,128]{2,1,0:T(8,128)S(1)} %get-tuple-element.22), custom_call_target="InvertDiagBlocksLowerTriangular" | custom-call | tf_op jit(solution)/shard_map/jit(_cho_solve)/triangular_solve | solution.py:10
  193.4 2.5 copy.83
  195.9 9.6 %fusion.2 = f32[256,4,512]{2,0,1:T(8,128)} fusion(bf16[16,256,512,1]{2,1,0,3:T(8,128)(2,1)S(1)} %bitcast.134, bf16[4,256,16,256]{3,2,1,0:T(8,128)(2,1)} %bitcast.136), kind=kOutput, calls=%fused_computation.6 | convolution fusion | flops 4294967296 | bytes 14680064 | tf_op jit(solution)/shard_map/axcy,cyz->xaz/dot_general | solution.py:49
  207.0 64.7 %all-reduce.5.cloned.1.call-done = f32[256,4,512]{2,0,1:T(8,128)} async-done(((f32[256,4,512]{2,0,1:T(8,128)}), f32[256,4,512]{2,0,1:T(8,128)}) %all-reduce.5.cloned.1.call-update) | async-done | bytes 2097168 | tf_op jit(solution)/shard_map/psum | solution.py:48
  271.7 1.0 fusion.15
  274.5 1.1 fusion.10
  275.6 0.9 convolution_bitcast_fusion.1
  276.8 1.6 fusion.71
  278.5 254.5 %all-reduce.7.cloned.1.call-done = (f32[256,256]{1,0:T(8,128)}, f32[256,256]{1,0:T(8,128)}, f32[256,256]{1,0:T(8,128)}) async-done(((f32[256,256]{1,0:T(8,128)}, f32[256,256]{1,0:T(8,128)}, f32[256,256]{1,0:T(8,128)}), (f32[256,256]{1,0:T(8,128)}, f32[256,256]{1,0:T(8,128)}, f32[256,256]{1,0:T(8,128)})) %all-reduce.7.cloned.1.call-update) | async-done | bytes 786448 | tf_op jit(solution)/shard_map/psum | solution.py:71
  533.0 1.0 maximum_subtract_fusion
  534.0 1.2 fusion.7
  535.2 1.9 fusion.6
  (77 shorter events, 17.8 us)
Async XLA Ops:
  7.2 267.4 %copy-start = (bf16[256,256]{1,0:T(8,128)(2,1)S(1)}, bf16[256,256]{1,0:T(8,128)(2,1)}, u32[]{:S(2)}) copy-start(bf16[256,256]{1,0:T(8,128)(2,1)} %param.16) | copy-start | bytes 393220
  7.2 87.6 %all-gather.3.cloned.1.call-start = ((), (), s32[]{:S(2)}) async-start(), calls=%async_computation.2 | async-start | bytes 4325376 | tf_op jit(solution)/shard_map/all_gather | solution.py:43
  99.5 93.9 %all-to-all-start = ((bf16[4,4,8,32,512]{4,3,1,0,2:T(8,128)(2,1)}), bf16[4,4,8,32,512]{4,3,1,0,2:T(8,128)(2,1)}, u32[]{:S(2)}, u32[]{:S(2)}) async-start(bf16[4,4,8,32,512]{4,3,1,0,2:T(8,128)(2,1)} %copy.82), calls=%async_computation | async-start | bytes 8388608 | tf_op jit(solution)/shard_map/all_to_all | solution.py:45
  107.4 164.3 %all-reduce.5.cloned.1.call-start = ((), (), s32[]{:S(2)}) async-start(), calls=%async_computation.1 | async-start | bytes 4194304 | tf_op jit(solution)/shard_map/psum | solution.py:48
  205.5 327.5 %all-reduce.7.cloned.1.call-start = ((), (), s32[]{:S(2)}) async-start(), calls=%async_computation.3 | async-start | bytes 1572864 | tf_op jit(solution)/shard_map/psum | solution.py:71
  275.6 261.5 %copy-start.3 = (bf16[32,4,256]{2,0,1:T(8,128)(2,1)}, bf16[32,4,256]{2,0,1:T(8,128)(2,1)S(1)}, u32[]{:S(2)}) copy-start(bf16[32,4,256]{2,0,1:T(8,128)(2,1)S(1)} %fusion.10) | copy-start | bytes 196612
  533.9 3.2 copy-start.1
  535.2 2.0 copy-start.2
Sparse Core Ops, SparseCore 0:
  11.6 83.1 all-gather.2
  205.6 66.0 all-reduce.4
  278.1 254.8 all-reduce.6
where the time goes:
time: 545 us; the launch traced here: 544 us
  waiting for transfers between devices  359 us (66%)
  other arithmetic  120 us (22%)
  matrix products  20.9 us (4%)
  local copies, waits for them, and re-layouts  18.6 us (3%)
  between operations  16.7 us (3%)
  starting transfers between devices  8 us (1%)
    psum x1, waiting for transfers between devices, per_device(): lax.psum((first_term, cross_term, second_term), ('prow', 'pcol'))  254 us
    another operation x14, other arithmetic, pivot_inverse(): factor = jnp.linalg.cholesky(h_block + shift * s_block)  69.2 us
    psum x1, waiting for transfers between devices, per_device(): lax.psum(jnp.einsum('axcy,cyz->xaz', inverse_rows, column_blocks, preferr...  64.7 us
    all_gather x1, waiting for transfers between devices, per_device(): gathered = lax.all_gather(stacked, 'prow', axis=1, tiled=True)  39.8 us
    another operation x5, other arithmetic, pivot_inverse(): return jax.scipy.linalg.cho_solve((factor, True), identity)  39.6 us
  transfers between devices with their start and end apart: 4, of which 3 were waited for; matrix products, arithmetic and copies ran while one was open for 24% of the time, Pallas kernels for 0%

commit v1 on v0

v1 whole, which is shorter than its diff:
```python
import jax
import jax.numpy as jnp
from jax import lax
from jax.experimental import pallas as pl
from jax.experimental.pallas import tpu as pltpu
from jax.sharding import PartitionSpec as P

MESH = pl.DeviceIdType.MESH
F32 = jnp.float32
BF16 = jnp.bfloat16
HI = lax.Precision.HIGHEST
NX, NZ, NY = 4, 8, 4
W = 256
BLK = 32


def sweep_block(x):
    n = x.shape[0]
    rows = lax.broadcasted_iota(jnp.int32, (n, n), 0)
    cols = lax.broadcasted_iota(jnp.int32, (n, n), 1)
    row1 = lax.broadcasted_iota(jnp.int32, (n, 1), 0)
    col1 = lax.broadcasted_iota(jnp.int32, (1, n), 1)
    for k in range(n):
        inv = 1.0 / x[k : k + 1, k : k + 1]
        right = jnp.where(col1 == k, 1.0, x[k : k + 1, :]) * inv
        left = jnp.where(row1 == k, 1.0, -x[:, k : k + 1])
        x = jnp.where((rows == k) | (cols == k), 0.0, x) + left * right
    return x


def body(
    anc,
    l1,
    l2,
    top,
    keep1,
    keep2,
    piv_h,
    piv_s,
    shifts,
    pole,
    fc_out,
    fd_out,
    link_out,
    sc_out,
    sd_out,
    abuf,
    a32,
    abf,
    m,
    lm,
    prod,
    r1,
    r2,
    g,
    gs,
    terms,
    w1,
    u,
    w2,
    w3,
    w4,
    wf,
    load_sem,
    sc_s,
    sc_r,
    sc_l,
    a1_s,
    a1_r,
    a2_s,
    a2_r,
    b1_s,
    b1_r,
    b2_s,
    b2_r,
    b3_s,
    b3_r,
    r1_s,
    r1_r,
    r2_s,
    r2_r,
    p1_s,
    p1_r,
    p2_s,
    p2_r,
    p3_s,
    p3_r,
    p4_s,
    p4_r,
    p5_s,
    p5_r,
):
    prow = lax.axis_index("prow")
    q = lax.axis_index("pcol")
    x, z = prow // NZ, prow % NZ
    y, core = q // 2, q % 2

    def dev(xx, zz, qq):
        return {"prow": xx * NZ + zz, "pcol": qq}

    def xr(d):
        return (x + d) % NX

    def zr(d):
        return (z + d) % NZ

    def remote(src, dst, ssem, rsem, target):
        return pltpu.make_async_remote_copy(
            src_ref=src, dst_ref=dst, send_sem=ssem, recv_sem=rsem, device_id=target, device_id_type=MESH
        )

    sent = []

    def send(src, dst, ssem, rsem, target):
        copy = remote(src, dst, ssem, rsem, target)
        copy.start()
        sent.append(copy)

    def arrived(dst, ssem, rsem):
        remote(dst, dst, ssem, rsem, dev(x, z, (q + 1) % 8)).wait_recv()

    loads = [pltpu.make_async_copy(piv_h.at[core], g, load_sem.at[4])]
    loads.append(pltpu.make_async_copy(piv_s.at[core], gs, load_sem.at[5]))
    for a in range(4):
        loads.append(pltpu.make_async_copy(anc.at[a], abuf.at[a], load_sem.at[a]))
    for copy in loads:
        copy.start()

    barrier = pltpu.get_barrier_semaphore()

    def greet(target):
        pl.semaphore_signal(barrier, inc=1, device_id=target, device_id_type=MESH)

    @pl.when(q != z)
    def _():
        for d in range(8):
            greet(dev(x, q, d))

    for d in range(1, 8):
        greet(dev(x, z, (q + d) % 8))
        greet(dev(x, zr(d), q))
    for d in range(1, 4):
        greet(dev(xr(d), z, q))

    flag1 = [keep1[a * (NX * NZ) + prow].astype(F32) for a in range(4)]
    flag2 = [flag1[a] * keep2[a * (NX * NZ) + prow].astype(F32) for a in range(4)]
    for a in range(4):
        lm[0, a] = (l1[a].astype(F32) * flag1[a]).astype(BF16).reshape(2, 16, W)
        lm[1, a] = (l2[a].astype(F32) * flag2[a]).astype(BF16).reshape(2, 16, W)

    pl.semaphore_wait(barrier, 24)

    for h in range(2):

        def whole(d, h=h):
            zz = zr(d)
            src = lm.at[h, zz // 2, zz % 2]
            dst = m.at[h, zz // 2, x, q, zz % 2]
            return remote(src, dst, sc_s.at[h, d], sc_r.at[h, q], dev(x, zz, z))

        @pl.when(q == z)
        def _(h=h):
            pltpu.make_async_copy(
                lm.at[h, z // 2, z % 2], m.at[h, z // 2, x, q, z % 2], sc_l.at[h]
            ).start()

        @pl.when(q != z)
        def _(whole=whole):
            whole(0).start()

        for d in range(1, 8):
            whole(d).start()

    def relayout(a):
        loads[2 + a].wait()

        def widen(i, _):
            rows = pl.ds(pl.multiple_of(i * 512, 512), 512)
            for s in range(2):
                a32[s, rows, :] = abuf[a, rows, s * 128 : (s + 1) * 128].astype(F32)
            return 0

        lax.fori_loop(0, 8, widen, 0)
        for c in range(16):
            for s in range(2):
                lanes = slice(c * W + s * 128, c * W + (s + 1) * 128)
                abf[a * W : (a + 1) * W, lanes] = a32[s, pl.ds(c, W, stride=16), :].astype(BF16)

    relayout(0)
    loads[0].wait()
    loads[1].wait()
    shift = shifts[pole[0]]
    g[...] = g[...] + shift * gs[...]

    def invert_step(k):
        rows = pl.ds(pl.multiple_of(k * BLK, BLK), BLK)
        panel = g[rows, :]
        unit = (
            lax.broadcasted_iota(jnp.int32, (BLK, W), 1)
            == lax.broadcasted_iota(jnp.int32, (BLK, W), 0) + k * BLK
        ).astype(F32)
        lanes = lax.broadcasted_iota(jnp.int32, (BLK, W), 1)
        inside = (lanes >= k * BLK) & (lanes < k * BLK + BLK)
        pivot = lax.dot_general(
            panel, unit, (((1,), (1,)), ((), ())), precision=HI, preferred_element_type=F32
        )
        solved = jnp.dot(
            sweep_block(pivot), jnp.where(inside, -unit, panel), precision=HI, preferred_element_type=F32
        )
        g[...] = g[...] - lax.dot_general(
            panel, solved + unit, (((0,), (0,)), ((), ())), precision=HI, preferred_element_type=F32
        )
        g[rows, :] = solved

    def invert(first, last):
        def step(k, _):
            invert_step(k)
            return 0

        lax.fori_loop(first, last, step, 0)

    lo, hi = pl.ds(0, 4), pl.ds(4, 4)

    def mine(h, zz, part):
        return m.at[h, zz // 2, x, part, zz % 2]

    def group(h, zz, s):
        return m.at[h, zz // 2, pl.ds(2 * s, 2), lo, zz % 2]

    def at_x(h, zz, xx):
        return m.at[h, zz // 2, xx, hi, zz % 2]

    def cross(h, d):
        zz = zr(d)
        send(mine(h, zz, hi), mine(h, zz, hi), b2_s.at[h, d % 8, 0], b2_r.at[h, d % 8, 0], dev(xr(1), z, q))
        send(mine(h, zz, hi), mine(h, zz, hi), b2_s.at[h, d % 8, 1], b2_r.at[h, d % 8, 1], dev(xr(3), z, q))

    def high_z(h, r):
        for i, step in enumerate((1, -1)):
            zz = zr(-step * (r - 1))
            if r < 4:
                part = hi
            else:
                part = pl.ds(4 + 2 * i, 2)
            ref = mine(h, zz, part)
            send(ref, ref, b1_s.at[h, r - 1, i], b1_r.at[h, r - 1, i], dev(x, zr(step), q))

    def high_z_wait(h, r):
        for i, step in enumerate((1, -1)):
            zz = zr(-step * r)
            part = hi if r < 4 else pl.ds(4 + 2 * i, 2)
            arrived(mine(h, zz, part), b1_s.at[h, r - 1, i], b1_r.at[h, r - 1, i])

    def low_z(h, r, s):
        for i, step in enumerate((1, -1)):
            if r == 4 and s != i:
                continue
            ref = group(h, zr(-step * (r - 1)), s)
            send(ref, ref, a2_s.at[h, r - 1, i, s], a2_r.at[h, r - 1, i, s], dev(x, zr(step), q))

    def low_z_wait(h, r, s):
        for i, step in enumerate((1, -1)):
            if r == 4 and s != i:
                continue
            arrived(group(h, zr(-step * r), s), a2_s.at[h, r - 1, i, s], a2_r.at[h, r - 1, i, s])

    def start(h):
        @pl.when(q == z)
        def _():
            pltpu.make_async_copy(
                lm.at[h, z // 2, z % 2], m.at[h, z // 2, x, q, z % 2], sc_l.at[h]
            ).wait()

        for d in range(8):
            src_q = (q + d) % 8
            dst = m.at[h, z // 2, x, src_q, z % 2]
            if d == 0:

                @pl.when(q != z)
                def _(dst=dst, src_q=src_q):
                    arrived(dst, sc_s.at[h, 0], sc_r.at[h, src_q])
            else:
                arrived(dst, sc_s.at[h, d], sc_r.at[h, src_q])
        for d in (1, 3, 2):
            ref = mine(h, z, lo)
            send(ref, ref, a1_s.at[h, d - 1], a1_r.at[h, d - 1], dev(xr(d), z, q))
        high_z(h, 1)
        cross(h, 0)

    def low_start(h):
        for d in (1, 3, 2):
            arrived(m.at[h, z // 2, xr(-d), lo, z % 2], a1_s.at[h, d - 1], a1_r.at[h, d - 1])
        for s in range(2):
            low_z(h, 1, s)

    def low(h, r):
        for s in range(2):
            low_z_wait(h, r, s)
            if r < 4:
                low_z(h, r + 1, s)

    def high(h, r):
        high_z_wait(h, r)
        if r < 4:
            high_z(h, r + 1)
            cross(h, r)
            cross(h, -r)
        else:
            cross(h, 4)

    def hop(h, d):
        zz = zr(d)
        slot = d % 8
        arrived(at_x(h, zz, xr(-1)), b2_s.at[h, slot, 0], b2_r.at[h, slot, 0])
        arrived(at_x(h, zz, xr(1)), b2_s.at[h, slot, 1], b2_r.at[h, slot, 1])
        if d in (0, 1, 2, -3):
            ref = at_x(h, zz, xr(-1))
            send(ref, ref, b3_s.at[h, slot], b3_r.at[h, slot], dev(xr(1), z, q))
        else:
            ref = at_x(h, zz, xr(1))
            send(ref, ref, b3_s.at[h, slot], b3_r.at[h, slot], dev(xr(3), z, q))

    def hop_wait(h):
        for d in range(8):
            arrived(at_x(h, zr(d), xr(2)), b3_s.at[h, d], b3_r.at[h, d])

    def multiply(h):
        def rows(a, _):
            weights = m[h].reshape(16 * W, W)
            part = jnp.dot(
                abf[pl.ds(pl.multiple_of(a * W, W), W), :], weights, preferred_element_type=F32
            )
            prod[h, a] = part.reshape(4, 2, 32, W)
            remote(
                prod.at[h, a, :, 1 - core],
                r1.at[h, a],
                r1_s.at[h, a],
                r1_r.at[h, a],
                dev(x, z, q + 1 - 2 * core),
            ).start()
            return 0

        lax.fori_loop(0, 4, rows, 0)

    def pair_sum(h):
        def rows(a, _):
            remote(
                prod.at[h, a, :, 1 - core],
                r1.at[h, a],
                r1_s.at[h, a],
                r1_r.at[h, a],
                dev(x, z, q + 1 - 2 * core),
            ).wait_recv()
            for yy in range(4):
                prod[h, a, yy, core] = prod[h, a, yy, core] + r1[h, a, yy]
            for d in (2, 1, 3):
                yy = (y + d) % NY
                remote(
                    prod.at[h, a, yy, core],
                    r2.at[h, d - 1, a],
                    r2_s.at[h, d - 1, a],
                    r2_r.at[h, d - 1, a],
                    dev(x, z, yy * 2 + core),
                ).start()
            return 0

        lax.fori_loop(0, 4, rows, 0)

    def y_copy(h, d, a):
        yy = (y + d) % NY
        return remote(
            prod.at[h, a, yy, core],
            r2.at[h, d - 1, a],
            r2_s.at[h, d - 1, a],
            r2_r.at[h, d - 1, a],
            dev(x, z, yy * 2 + core),
        )

    def row_part(h, a):
        total = prod[h, a, y, core]
        for d in (1, 2, 3):
            y_copy(h, d, a).wait_recv()
            total = total + r2[h, d - 1, a]
        return total

    def finish_first():
        for a in range(4):
            fc_out[a] = (-row_part(0, a) * flag1[a]).astype(BF16)

    def finish_second():
        for a in range(4):
            bridge = jnp.dot(fc_out[a], top[...], preferred_element_type=F32)
            sc_out[a] = (-(row_part(1, a) + bridge) * flag2[a]).astype(BF16)

    start(0)
    low_start(0)
    high(0, 1)
    relayout(1)
    high(0, 2)
    start(1)
    low(0, 1)
    high(0, 3)
    hop(0, 0)
    high(0, 4)
    hop(0, 1)
    hop(0, -1)
    relayout(2)
    low(0, 2)
    low_start(1)
    high(1, 1)
    hop(0, 2)
    hop(0, -2)
    high(1, 2)
    relayout(3)
    low(0, 3)
    hop(0, 3)
    hop(0, -3)
    hop(0, 4)
    high(1, 3)
    low(0, 4)
    low(1, 1)
    high(1, 4)
    hop_wait(0)
    multiply(0)
    for d in (0, 1, -1, 2, -2):
        hop(1, d)
    low(1, 2)
    pair_sum(0)
    for d in (3, -3, 4):
        hop(1, d)
    invert(0, 1)
    low(1, 3)
    finish_first()
    invert(1, 2)
    low(1, 4)
    hop_wait(1)
    multiply(1)
    pair_sum(1)
    invert(2, 8)
    finish_second()

    def contract(left, right):
        return lax.dot_general(left, right, (((0,), (0,)), ((), ())), preferred_element_type=F32)

    lower1 = lm[0].reshape(128, W)
    lower2 = lm[1].reshape(128, W)
    first = fc_out[...].reshape(128, W)
    second = sc_out[...].reshape(128, W)
    owner1 = ((prow == 0) & (q == 0)).astype(F32)
    owner2 = ((prow == 0) & (q == 1)).astype(F32)
    terms[:, 0] = (contract(lower1, first) + owner1 * g[...]).reshape(8, 32, W)
    terms[:, 1] = contract(first, lower2).reshape(8, 32, W)
    terms[:, 2] = (contract(lower2, second) + owner2 * g[...]).reshape(8, 32, W)

    for d in range(1, 8):
        qq = (q + d) % 8
        send(terms.at[qq], w1.at[d - 1], p1_s.at[d - 1], p1_r.at[d - 1], dev(x, z, qq))
    total = terms[q]
    for d in range(1, 8):
        arrived(w1.at[d - 1], p1_s.at[d - 1], p1_r.at[d - 1])
        total = total + w1[d - 1]
    for xx in range(4):
        u[xx] = total[:, xx * 8 : (xx + 1) * 8, :]
    for d in range(1, 4):
        send(u.at[xr(d)], w2.at[d - 1], p2_s.at[d - 1], p2_r.at[d - 1], dev(xr(d), z, q))
    total = u[x]
    for d in range(1, 4):
        arrived(w2.at[d - 1], p2_s.at[d - 1], p2_r.at[d - 1])
        total = total + w2[d - 1]
    w3[z] = total
    for d in range(1, 8):
        send(w3.at[z], w3.at[z], p3_s.at[d - 1], p3_r.at[d - 1], dev(x, zr(d), q))
    for d in range(1, 8):
        arrived(w3.at[zr(-d)], p3_s.at[d - 1], p3_r.at[d - 1])
    total = w3[0]
    for zz in range(1, 8):
        total = total + w3[zz]
    w4[x] = total
    for d in range(1, 4):
        send(w4.at[x], w4.at[x], p4_s.at[d - 1], p4_r.at[d - 1], dev(xr(d), z, q))
    for d in range(1, 4):
        arrived(w4.at[xr(-d)], p4_s.at[d - 1], p4_r.at[d - 1])
    for d in range(1, 8):
        send(w4, wf.at[q], p5_s.at[d - 1], p5_r.at[d - 1], dev(x, z, (q + d) % 8))
    wf[q] = w4[...]
    for d in range(1, 8):
        arrived(wf.at[(q - d) % 8], p5_s.at[d - 1], p5_r.at[d - 1])

    first_diag = -wf[:, :, 0].reshape(W, W)
    fd_out[...] = first_diag
    link = -(
        wf[:, :, 1].reshape(W, W)
        + jnp.dot(first_diag.astype(BF16), top[...], preferred_element_type=F32)
    )
    link = link.astype(BF16)
    link_out[...] = link
    sd_out[...] = -wf[:, :, 2].reshape(W, W) - contract(top[...], link)

    for copy in sent:
        copy.wait_send()
    for h in range(2):

        @pl.when(q != z)
        def _(h=h):
            remote(
                lm.at[h, z // 2, z % 2],
                m.at[h, z // 2, x, q, z % 2],
                sc_s.at[h, 0],
                sc_r.at[h, q],
                dev(x, z, z),
            ).wait_send()

        for d in range(1, 8):
            zz = zr(d)
            remote(
                lm.at[h, zz // 2, zz % 2],
                m.at[h, zz // 2, x, q, zz % 2],
                sc_s.at[h, d],
                sc_r.at[h, q],
                dev(x, zz, z),
            ).wait_send()
        for a in range(4):
            remote(
                prod.at[h, a, :, 1 - core],
                r1.at[h, a],
                r1_s.at[h, a],
                r1_r.at[h, a],
                dev(x, z, q + 1 - 2 * core),
            ).wait_send()
            for d in (1, 2, 3):
                y_copy(h, d, a).wait_send()


def per_device(
    anc_inverse,
    first_lower,
    second_lower,
    second_top,
    struct_first,
    struct_keep,
    pivot_h,
    pivot_s,
    shifts,
    pole_index,
):
    vmem = pl.BlockSpec(memory_space=pltpu.VMEM)
    smem = pl.BlockSpec(memory_space=pltpu.SMEM)
    hbm = pl.BlockSpec(memory_space=pl.ANY)
    dma = pltpu.SemaphoreType.DMA
    fc, fd, link, sc, sd = pl.pallas_call(
        body,
        out_shape=(
            jax.ShapeDtypeStruct((4, 32, W), BF16),
            jax.ShapeDtypeStruct((W, W), F32),
            jax.ShapeDtypeStruct((W, W), BF16),
            jax.ShapeDtypeStruct((4, 32, W), BF16),
            jax.ShapeDtypeStruct((W, W), F32),
        ),
        in_specs=[hbm, vmem, vmem, vmem, smem, smem, hbm, hbm, smem, smem],
        out_specs=(vmem,) * 5,
        scratch_shapes=[
            pltpu.VMEM((4, 4096, W), BF16),
            pltpu.VMEM((2, 4096, 128), F32),
            pltpu.VMEM((1024, 4096), BF16),
            pltpu.VMEM((2, 4, 4, 8, 2, 16, W), BF16),
            pltpu.VMEM((2, 4, 2, 16, W), BF16),
            pltpu.VMEM((2, 4, 4, 2, 32, W), F32),
            pltpu.VMEM((2, 4, 4, 32, W), F32),
            pltpu.VMEM((2, 3, 4, 32, W), F32),
            pltpu.VMEM((W, W), F32),
            pltpu.VMEM((W, W), F32),
            pltpu.VMEM((8, 3, 32, W), F32),
            pltpu.VMEM((7, 3, 32, W), F32),
            pltpu.VMEM((4, 3, 8, W), F32),
            pltpu.VMEM((3, 3, 8, W), F32),
            pltpu.VMEM((8, 3, 8, W), F32),
            pltpu.VMEM((4, 3, 8, W), F32),
            pltpu.VMEM((8, 4, 3, 8, W), F32),
            dma((6,)),
            dma((2, 8)),
            dma((2, 8)),
            dma((2,)),
            dma((2, 3)),
            dma((2, 3)),
            dma((2, 4, 2, 2)),
            dma((2, 4, 2, 2)),
            dma((2, 4, 2)),
            dma((2, 4, 2)),
            dma((2, 8, 2)),
            dma((2, 8, 2)),
            dma((2, 8)),
            dma((2, 8)),
            dma((2, 4)),
            dma((2, 4)),
            dma((2, 3, 4)),
            dma((2, 3, 4)),
            dma((7,)),
            dma((7,)),
            dma((3,)),
            dma((3,)),
            dma((7,)),
            dma((7,)),
            dma((3,)),
            dma((3,)),
            dma((7,)),
            dma((7,)),
        ],
        compiler_params=pltpu.CompilerParams(
            collective_id=0, has_side_effects=True, vmem_limit_bytes=56 * 1024 * 1024
        ),
        name="selected_inversion",
    )(
        anc_inverse.reshape(4, 4096, W),
        first_lower.reshape(4, 32, W),
        second_lower.reshape(4, 32, W),
        second_top,
        struct_first,
        struct_keep,
        pivot_h,
        pivot_s,
        shifts,
        pole_index,
    )
    return fc[:, None], fd, link, sc[:, None], sd


def solution(mesh):
    return jax.shard_map(
        per_device,
        mesh=mesh,
        in_specs=(
            P(None, "prow", None, None, "pcol", None),
            P(None, "prow", "pcol", None),
            P(None, "prow", "pcol", None),
            P(),
            P(),
            P(),
            P(),
            P(),
            P(),
            P(),
        ),
        out_specs=(P(None, "prow", "pcol", None), P(), P(), P(None, "prow", "pcol", None), P()),
        check_vma=False,
    )
```

time: 545 us -> 139 us (0.26)
  waiting for transfers between devices: 359 us -> 0 us
  Pallas kernels: 0 us -> 130 us
  other arithmetic: 120 us -> 0 us
  matrix products: 20.9 us -> 0 us
  between operations: 16.7 us -> 0.65 us
  local copies, waits for them, and re-layouts: 18.6 us -> 7.85 us
  starting transfers between devices: 8 us -> 0 us
    psum x2 -> x0, waiting for transfers between devices: 319 us -> none  [the longest x1 254 us: per_device(): lax.psum((first_term, cross_term, second_term), ('prow', 'pcol'))]
    pallas_call x0 -> x1, Pallas kernels: none -> 130 us  [per_device(): pl.pallas_call(body, out_shape=(jax.ShapeDtypeStruct((4, 32, W), BF16), j...]
    another operation x19 -> x0, other arithmetic: 109 us -> none  [the longest x14 69.2 us: pivot_inverse(): factor = jnp.linalg.cholesky(h_block + shift * s_block)]
    all_gather x1 -> x0, waiting for transfers between devices: 39.8 us -> none  [per_device(): gathered = lax.all_gather(stacked, 'prow', axis=1, tiled=True)]
    dot_general x7 -> x0, matrix products: 16.6 us -> none  [the longest x1 9.58 us: per_device(): jnp.einsum('axcy,cyz->xaz', inverse_rows, column_blocks, preferred_elemen...]
    another operation x19 -> x0, local copies, waits for them, and re-layouts: 8.04 us -> none  [the longest x15 7.99 us: pivot_inverse(): return jax.scipy.linalg.cho_solve((factor, True), identity)]
    all_to_all x1 -> x0, starting transfers between devices: 7.92 us -> none  [per_device(): lax.all_to_all(grouped, 'pcol', split_axis=2, concat_axis=3, tiled=True)]
    unnamed x12 -> x5, local copies, waits for them, and re-layouts: 0.54 us -> 7.85 us
  transfers between devices with their start and end apart: 4 -> 0, of which waited for: 3 -> 0; matrix products, arithmetic and copies ran while one was open for 24% -> 0% of each run, Pallas kernels for 0% -> 0%
where the time goes in v1:
time: 139 us
  Pallas kernels  130 us (94%)
  local copies, waits for them, and re-layouts  7.85 us (6%)
    pallas_call x1, Pallas kernels, per_device(): pl.pallas_call(body, out_shape=(jax.ShapeDtypeStruct((4, 32, W), BF16), j...  130 us
    unnamed x5, local copies, waits for them, and re-layouts  7.85 us

profile of v1, /device:TPU:1, one launch (start us, length us, event | category | flops | bytes accessed | tf_op | source)
XLA Modules:
  0.0 138.7 jit_solution(11499561846500639022)
XLA Ops:
  0.6 130.2 %selected_inversion.1 = (bf16[4,32,256]{2,1,0:T(8,128)(2,1)}, f32[256,256]{1,0:T(8,128)}, bf16[256,256]{1,0:T(8,128)(2,1)}, bf16[4,32,256]{2,1,0:T(8,128)(2,1)}, f32[256,256]{1,0:T(8,128)}) custom-call(bf16[4,4096,256]{2,1,0:T(8,128)(2,1)} %bitcast.9, bf16[4,32,256]{2,1,0:T(8,128)(2,1)} %bitcast.10, bf16[4,32,256]{2,1,0:T(8,128)(2,1)} %bitcast.11, ...), custom_call_target="tpu_custom_call" | custom-call | tf_op jit(solution)/shard_map/selected_inversion/pallas_call | solution.py:550
  130.8 1.5 %copy.22 = bf16[4,1,32,256]{3,2,1,0:T(8,128)(2,1)} copy(bf16[4,1,32,256]{3,2,1,0:T(8,128)(2,1)} %bitcast.13) | data formatting | bytes 131072
  132.3 1.7 %copy.23 = f32[256,256]{1,0:T(8,128)} copy(f32[256,256]{1,0:T(8,128)} %get-tuple-element.26) | data formatting | bytes 524288
  133.9 1.6 %copy.24 = bf16[256,256]{1,0:T(8,128)(2,1)} copy(bf16[256,256]{1,0:T(8,128)(2,1)} %get-tuple-element.27) | data formatting | bytes 262144
  135.5 1.5 %copy.25 = bf16[4,1,32,256]{3,2,1,0:T(8,128)(2,1)} copy(bf16[4,1,32,256]{3,2,1,0:T(8,128)(2,1)} %bitcast.12) | data formatting | bytes 131072
  137.0 1.7 %copy.26 = f32[256,256]{1,0:T(8,128)} copy(f32[256,256]{1,0:T(8,128)} %get-tuple-element.29) | data formatting | bytes 524288

commit v2 on v0

v2 whole, which is shorter than its diff:
```python
import jax
import jax.numpy as jnp
from jax import lax
from jax.experimental import pallas as pl
from jax.experimental.pallas import tpu as pltpu
from jax.sharding import PartitionSpec as P

MESH = pl.DeviceIdType.MESH
F32 = jnp.float32
BF16 = jnp.bfloat16
HI = lax.Precision.HIGHEST
NX, NZ, NY = 4, 8, 4
W = 256
BLK = 32
LOW = 3


def gauss_jordan(x, first, last):
    n = x.shape[0]
    rows = lax.broadcasted_iota(jnp.int32, (n, n), 0)
    cols = lax.broadcasted_iota(jnp.int32, (n, n), 1)
    row1 = lax.broadcasted_iota(jnp.int32, (n, 1), 0)
    col1 = lax.broadcasted_iota(jnp.int32, (1, n), 1)
    for k in range(first, last):
        inv = 1.0 / x[k : k + 1, k : k + 1]
        right = jnp.where(col1 == k, 1.0, x[k : k + 1, :]) * inv
        left = jnp.where(row1 == k, 1.0, -x[:, k : k + 1])
        x = jnp.where((rows == k) | (cols == k), 0.0, x) + left * right
    return x


def contract(left, right):
    return lax.dot_general(left, right, (((0,), (0,)), ((), ())), preferred_element_type=F32)


def split(value):
    high = value.astype(BF16)
    return high, (value - high.astype(F32)).astype(BF16)


def body(
    anc,
    l1,
    l2,
    top_in,
    keep1_in,
    keep2_in,
    piv_h,
    piv_s,
    shifts_in,
    pole_in,
    fc_out,
    fd_out,
    link_out,
    sc_out,
    sd_out,
    abuf,
    a32,
    abf,
    m,
    ll,
    lm,
    mb,
    mbt,
    prod,
    r1,
    r2,
    g,
    gs,
    gp,
    fc,
    sc,
    fd,
    link,
    sd,
    top,
    keep1,
    keep2,
    shifts,
    pole,
    ta,
    wa0,
    ua,
    wa1,
    wa3,
    wa4,
    waf,
    tb,
    wb0,
    ub,
    wb1,
    wb3,
    wb4,
    wbf,
    load_sem,
    out_sem,
    sc_s,
    sc_r,
    sc_l,
    mb_s,
    mb_r,
    a1_s,
    a1_r,
    a2_s,
    a2_r,
    b1_s,
    b1_r,
    b2_s,
    b2_r,
    b3_s,
    b3_r,
    r1_s,
    r1_r,
    r2_s,
    r2_r,
    p_s,
    p_r,
):
    prow = lax.axis_index("prow")
    q = lax.axis_index("pcol")
    x, z = prow // NZ, prow % NZ
    y, core = q // 2, q % 2

    def dev(xx, zz, qq):
        return {"prow": xx * NZ + zz, "pcol": qq}

    def xr(d):
        return (x + d) % NX

    def zr(d):
        return (z + d) % NZ

    def qr(d):
        return (q + d) % 8

    barrier = pltpu.get_barrier_semaphore()

    def greet(target):
        pl.semaphore_signal(barrier, inc=1, device_id=target, device_id_type=MESH)

    @pl.when(q != z)
    def _():
        for d in range(8):
            greet(dev(x, q, d))

    for d in range(1, 8):
        greet(dev(x, z, qr(d)))
        greet(dev(x, zr(d), q))
    for dx in range(1, 4):
        for dy in range(4):
            greet(dev(xr(dx), z, qr(2 * dy)))

    def load(src, dst, i):
        copy = pltpu.make_async_copy(src, dst, load_sem.at[i])
        copy.start()
        return copy

    factors = [load(l1, ll.at[0], 0), load(l2, ll.at[1], 1)]
    flags = [load(keep1_in, keep1, 2), load(keep2_in, keep2, 3)]
    pivots = [load(piv_h.at[core], g, 4), load(piv_s.at[core], gs, 5)]
    pivots += [load(shifts_in, shifts, 6), load(pole_in, pole, 7)]
    tops = load(top_in, top, 8)
    blocks = [load(anc.at[a], abuf.at[a], 9 + a) for a in range(4)]

    def remote(src, dst, ssem, rsem, target):
        return pltpu.make_async_remote_copy(
            src_ref=src, dst_ref=dst, send_sem=ssem, recv_sem=rsem, device_id=target, device_id_type=MESH
        )

    sent = []

    def send(src, dst, ssem, rsem, target):
        copy = remote(src, dst, ssem, rsem, target)
        copy.start()
        sent.append(copy)

    def arrived(dst, ssem, rsem):
        remote(dst, dst, ssem, rsem, dev(x, z, qr(1))).wait_recv()

    for copy in factors + flags:
        copy.wait()
    flag1 = [keep1[a * (NX * NZ) + prow].astype(F32) for a in range(4)]
    flag2 = [flag1[a] * keep2[a * (NX * NZ) + prow].astype(F32) for a in range(4)]
    for a in range(4):
        lm[0, a] = (ll[0, a].astype(F32) * flag1[a]).astype(BF16)
        lm[1, a] = (ll[1, a].astype(F32) * flag2[a]).astype(BF16)

    pl.semaphore_wait(barrier, 33)

    def slice_of(zz):
        return lm.at[:, zz // 2, pl.ds(pl.multiple_of(16 * (zz % 2), 16), 16)]

    def spread(d):
        zz = zr(d)
        dst = m.at[:, zz // 2, x, q, zz % 2]
        return remote(slice_of(zz), dst, sc_s.at[d], sc_r.at[q], dev(x, zz, z))

    def keep_own():
        return pltpu.make_async_copy(slice_of(z), m.at[:, z // 2, x, q, z % 2], sc_l)

    @pl.when(q == z)
    def _():
        keep_own().start()

    @pl.when(q != z)
    def _():
        spread(0).start()

    for d in range(1, 8):
        spread(d).start()

    def relayout(a):
        blocks[a].wait()

        def widen(i, _):
            rows = pl.ds(pl.multiple_of(i * 512, 512), 512)
            for s in range(2):
                a32[s, rows, :] = abuf[a, rows, s * 128 : (s + 1) * 128].astype(F32)
            return 0

        lax.fori_loop(0, 8, widen, 0)

        def pick(c, _):
            for s in range(2):
                lanes = pl.ds(pl.multiple_of(c * W + s * 128, 128), 128)
                abf[a * W : (a + 1) * W, lanes] = a32[s, pl.ds(c, W, stride=16), :].astype(BF16)
            return 0

        lax.fori_loop(0, 16, pick, 0)

    def inverse_pieces():
        for k in range(W // BLK):
            rows = pl.ds(k * BLK, BLK)
            for part in range(4):
                block = g[rows, k * BLK : (k + 1) * BLK] if part == 0 else gp[...]
                gp[...] = gauss_jordan(block, part * 8, part * 8 + 8)
                yield
            panel = g[rows, :]
            lanes = lax.broadcasted_iota(jnp.int32, (BLK, W), 1)
            unit = (lanes == lax.broadcasted_iota(jnp.int32, (BLK, W), 0) + k * BLK).astype(F32)
            inside = (lanes >= k * BLK) & (lanes < k * BLK + BLK)
            solved = jnp.dot(
                gp[...], jnp.where(inside, -unit, panel), precision=HI, preferred_element_type=F32
            )
            g[...] = g[...] - lax.dot_general(
                panel, solved + unit, (((0,), (0,)), ((), ())), precision=HI, preferred_element_type=F32
            )
            g[rows, :] = solved
            yield

    pieces = inverse_pieces()

    def work(n):
        for _ in range(n):
            next(pieces, None)

    relayout(0)
    for copy in pivots:
        copy.wait()
    g[...] = g[...] + shifts[pole[0]] * gs[...]

    lo, hi = pl.ds(0, LOW), pl.ds(LOW, 8 - LOW)

    def mine(h, zz, part):
        return m.at[h, zz // 2, x, part, zz % 2]

    def group(h, zz, s):
        return m.at[h, zz // 2, pl.ds(2 * s, 2), lo, zz % 2]

    def at_x(h, zz, xx):
        return m.at[h, zz // 2, xx, hi, zz % 2]

    def cross(h, d):
        ref = mine(h, zr(d), hi)
        send(ref, ref, b2_s.at[h, d % 8, 0], b2_r.at[h, d % 8, 0], dev(xr(1), z, q))
        send(ref, ref, b2_s.at[h, d % 8, 1], b2_r.at[h, d % 8, 1], dev(xr(3), z, q))

    def far(i):
        half = (8 - LOW + 1) // 2
        return pl.ds(LOW, half) if i == 0 else pl.ds(LOW + half, 8 - LOW - half)

    def high_first(h):
        ref = mine(h, z, hi)
        for e in (1, -1, 2, -2):
            slot = -e % 8
            send(ref, ref, b1_s.at[h, slot], b1_r.at[h, slot], dev(x, zr(e), q))

    def high_second(h):
        for i, step in enumerate((1, -1)):
            zz = zr(-2 * step)
            slot = -2 * step % 8
            ref = mine(h, zz, hi)
            arrived(ref, b1_s.at[h, slot], b1_r.at[h, slot])
            slot = -3 * step % 8
            send(ref, ref, b1_s.at[h, slot], b1_r.at[h, slot], dev(x, zr(step), q))
            slot = 4 if i == 0 else 0
            ref = mine(h, zz, far(i))
            send(ref, ref, b1_s.at[h, slot], b1_r.at[h, slot], dev(x, zr(2 * step), q))
        for d in (1, -1):
            arrived(mine(h, zr(d), hi), b1_s.at[h, d % 8], b1_r.at[h, d % 8])
        for d in (1, -1, 2, -2):
            cross(h, d)

    def high_third(h):
        for d in (3, -3):
            arrived(mine(h, zr(d), hi), b1_s.at[h, d % 8], b1_r.at[h, d % 8])
            cross(h, d)
        for i, slot in enumerate((4, 0)):
            arrived(mine(h, zr(4), far(i)), b1_s.at[h, slot], b1_r.at[h, slot])
        cross(h, 4)

    def low_z(h, r, s):
        for i, step in enumerate((1, -1)):
            if r == 4 and s != i:
                continue
            ref = group(h, zr(-step * (r - 1)), s)
            send(ref, ref, a2_s.at[h, r - 1, i, s], a2_r.at[h, r - 1, i, s], dev(x, zr(step), q))

    def low_z_wait(h, r, s):
        for i, step in enumerate((1, -1)):
            if r == 4 and s != i:
                continue
            arrived(group(h, zr(-step * r), s), a2_s.at[h, r - 1, i, s], a2_r.at[h, r - 1, i, s])

    def begin():
        @pl.when(q == z)
        def _():
            keep_own().wait()

        @pl.when(q != z)
        def _():
            arrived(m.at[:, z // 2, x, q, z % 2], sc_s.at[0], sc_r.at[q])

        for d in range(1, 8):
            arrived(m.at[:, z // 2, x, qr(d), z % 2], sc_s.at[d], sc_r.at[qr(d)])

    def first_sends(h):
        for d in (1, 3, 2):
            ref = mine(h, z, lo)
            send(ref, ref, a1_s.at[h, d - 1], a1_r.at[h, d - 1], dev(xr(d), z, q))
        high_first(h)
        cross(h, 0)

    def low_start(h):
        for d in (1, 3, 2):
            arrived(m.at[h, z // 2, xr(-d), lo, z % 2], a1_s.at[h, d - 1], a1_r.at[h, d - 1])
        for s in range(2):
            low_z(h, 1, s)

    def low(h, r):
        for s in range(2):
            low_z_wait(h, r, s)
            if r < 4:
                low_z(h, r + 1, s)

    def hop(h, *offsets):
        for d in offsets:
            zz = zr(d)
            slot = d % 8
            arrived(at_x(h, zz, xr(-1)), b2_s.at[h, slot, 0], b2_r.at[h, slot, 0])
            arrived(at_x(h, zz, xr(1)), b2_s.at[h, slot, 1], b2_r.at[h, slot, 1])
            if d in (0, 1, 2, -3):
                ref = at_x(h, zz, xr(-1))
                send(ref, ref, b3_s.at[h, slot], b3_r.at[h, slot], dev(xr(1), z, q))
            else:
                ref = at_x(h, zz, xr(1))
                send(ref, ref, b3_s.at[h, slot], b3_r.at[h, slot], dev(xr(3), z, q))

    def hop_wait(h):
        for d in range(8):
            arrived(at_x(h, zr(d), xr(2)), b3_s.at[h, d], b3_r.at[h, d])

    def pair_copy(h, a):
        return remote(
            prod.at[h, a, :, 1 - core],
            r1.at[h, a],
            r1_s.at[h, a],
            r1_r.at[h, a],
            dev(x, z, q + 1 - 2 * core),
        )

    def y_copy(h, d, a):
        yy = (y + d) % NY
        return remote(
            prod.at[h, a, yy, core],
            r2.at[h, d - 1, a],
            r2_s.at[h, d - 1, a],
            r2_r.at[h, d - 1, a],
            dev(x, z, yy * 2 + core),
        )

    def multiply(h):
        def rows(a, _):
            weights = m[h].reshape(16 * W, W)
            part = jnp.dot(
                abf[pl.ds(pl.multiple_of(a * W, W), W), :], weights, preferred_element_type=F32
            )
            prod[h, a] = part.reshape(4, 2, 32, W)
            pair_copy(h, a).start()
            return 0

        lax.fori_loop(0, 4, rows, 0)

    def pair_sum(h):
        def rows(a, _):
            pair_copy(h, a).wait_recv()
            for yy in range(4):
                prod[h, a, yy, core] = prod[h, a, yy, core] + r1[h, a, yy]
            for d in (2, 1, 3):
                y_copy(h, d, a).start()
            return 0

        lax.fori_loop(0, 4, rows, 0)

    def row_part(h, a):
        total = prod[h, a, y, core]
        for d in (1, 2, 3):
            y_copy(h, d, a).wait_recv()
            total = total + r2[h, d - 1, a]
        return total

    outs = []

    def put(src, dst, i):
        copy = pltpu.make_async_copy(src, dst, out_sem.at[i])
        copy.start()
        outs.append(copy)

    def finish_first():
        for a in range(4):
            fc[a] = (-row_part(0, a) * flag1[a]).astype(BF16)
        put(fc, fc_out, 0)

    def finish_second():
        for a in range(4):
            bridge = jnp.dot(fc[a], top[...], preferred_element_type=F32)
            sc[a] = (-(row_part(1, a) + bridge) * flag2[a]).astype(BF16)
        put(sc, sc_out, 1)

    def share_rows():
        for d in range(1, 8):
            send(lm.at[1], mb.at[:, q], mb_s.at[d - 1], mb_r.at[d - 1], dev(x, z, qr(d)))
        for a in range(4):
            mb[a, q] = lm[1, a]

    def turn_rows():
        for d in range(1, 8):
            arrived(mb.at[:, qr(-d)], mb_s.at[d - 1], mb_r.at[d - 1])
        for a in range(4):
            mbt[a] = mb[a].reshape(W, W).T

    spot = x * NY + y
    others = [(dx, dy) for dx in range(NX) for dy in range(NY) if dx or dy]

    def plane(dx, dy):
        xx, yy = (x + dx) % NX, (y + dy) % NY
        return xx * NY + yy, dev(xx, z, yy * 2 + core)

    def all_reduce(base, t, w0, u, w1, w3, w4, wf):
        def sems(i):
            return p_s.at[base + i], p_r.at[base + i]

        twin = dev(x, z, q + 1 - 2 * core)
        send(t.at[1 - core], w0, *sems(0), twin)
        yield
        arrived(w0, *sems(0))
        u[...] = t[core] + w0[...]
        for i, (dx, dy) in enumerate(others):
            there, target = plane(dx, dy)
            send(u.at[there], w1.at[i], *sems(1 + i), target)
        yield
        total = u[spot]
        for i in range(15):
            arrived(w1.at[i], *sems(1 + i))
            total = total + w1[i]
        w3[z] = total
        for d in range(1, 8):
            send(w3.at[z], w3.at[z], *sems(15 + d), dev(x, zr(d), q))
        yield
        for d in range(1, 8):
            arrived(w3.at[zr(-d)], *sems(15 + d))
        total = w3[0]
        for zz in range(1, 8):
            total = total + w3[zz]
        w4[spot] = total
        for i, (dx, dy) in enumerate(others):
            send(w4.at[spot], w4.at[spot], *sems(23 + i), plane(dx, dy)[1])
        yield
        for i, (dx, dy) in enumerate(others):
            arrived(w4.at[plane(-dx, -dy)[0]], *sems(23 + i))
        send(w4, wf.at[core], *sems(38), twin)
        wf[core] = w4[...]
        yield
        arrived(wf.at[1 - core], *sems(38))
        yield

    reduce_a = all_reduce(0, ta, wa0, ua, wa1, wa3, wa4, waf)
    reduce_b = all_reduce(39, tb, wb0, ub, wb1, wb3, wb4, wbf)

    relayout(1)
    relayout(2)
    begin()
    first_sends(0)
    share_rows()
    relayout(3)
    work(1)
    low_start(0)
    work(1)
    high_second(0)
    work(3)
    low(0, 1)
    high_third(0)
    first_sends(1)
    hop(0, 0, 1, -1, 2, -2)
    work(3)
    low(0, 2)
    low_start(1)
    high_second(1)
    hop(0, 3, -3, 4)
    work(4)
    low(0, 3)
    work(2)
    low(1, 1)
    high_third(1)
    work(2)
    low(0, 4)
    hop_wait(0)
    multiply(0)
    hop(1, 0, 1, -1, 2, -2)
    low(1, 2)
    pair_sum(0)
    hop(1, 3, -3, 4)
    work(6)
    low(1, 3)
    turn_rows()
    work(6)
    low(1, 4)
    hop_wait(1)
    multiply(1)

    owner1 = ((prow == 0) & (q == 0)).astype(F32)
    owner2 = ((prow == 0) & (q == 1)).astype(F32)

    def second_term():
        total = jnp.zeros((W, W), F32)
        for a in range(4):
            for piece in split(prod[1, a].reshape(W, W)):
                total = total + jnp.dot(mbt[a], piece, preferred_element_type=F32)
        return total

    work(40)
    tb[...] = (second_term() - owner2 * g[...]).reshape(2, 16, 1, 8, W)
    next(reduce_b)
    tops.wait()
    finish_first()
    first = fc[...].reshape(128, W)
    ta[:, :, 0] = (contract(lm[0].reshape(128, W), first) + owner1 * g[...]).reshape(2, 16, 8, W)
    ta[:, :, 1] = contract(first, lm[1].reshape(128, W)).reshape(2, 16, 8, W)
    next(reduce_a)
    next(reduce_b)
    next(reduce_a)
    pair_sum(1)
    next(reduce_b)
    next(reduce_a)
    next(reduce_b)
    next(reduce_a)
    finish_second()
    next(reduce_b)
    next(reduce_a)
    next(reduce_a)
    first_diag = -waf[:, :, 0].reshape(W, W)
    fd[...] = first_diag
    put(fd, fd_out, 2)
    cross_sum = waf[:, :, 1].reshape(W, W)
    lower = jnp.dot(first_diag.astype(BF16), top[...], preferred_element_type=F32)
    link[...] = (-(cross_sum + lower)).astype(BF16)
    put(link, link_out, 3)
    tail = -contract(top[...], link[...])
    for piece in split(cross_sum):
        tail = tail + contract(piece, top[...])
    next(reduce_b)
    sd[...] = wbf[:, :, 0].reshape(W, W) + tail
    put(sd, sd_out, 4)

    for copy in sent:
        copy.wait_send()

    @pl.when(q != z)
    def _():
        spread(0).wait_send()

    for d in range(1, 8):
        spread(d).wait_send()
    for h in range(2):
        for a in range(4):
            pair_copy(h, a).wait_send()
            for d in (1, 2, 3):
                y_copy(h, d, a).wait_send()
    for copy in outs:
        copy.wait()


def hand_out(*refs):
    ins, outs, stage, sem = refs[:5], refs[5:10], refs[10:15], refs[15]
    loads = [pltpu.make_async_copy(ins[i], stage[i], sem.at[i]) for i in range(5)]
    stores = [pltpu.make_async_copy(stage[i], outs[i], sem.at[5 + i]) for i in range(5)]
    for copy in loads:
        copy.start()
    for load, store in zip(loads, stores):
        load.wait()
        store.start()
    for copy in stores:
        copy.wait()


def per_device(
    anc_inverse,
    first_lower,
    second_lower,
    second_top,
    struct_first,
    struct_keep,
    pivot_h,
    pivot_s,
    shifts,
    pole_index,
):
    hbm = pl.BlockSpec(memory_space=pl.ANY)
    dma = pltpu.SemaphoreType.DMA
    vmem = pltpu.VMEM
    shapes = (
        jax.ShapeDtypeStruct((4, 32, W), BF16),
        jax.ShapeDtypeStruct((W, W), F32),
        jax.ShapeDtypeStruct((W, W), BF16),
        jax.ShapeDtypeStruct((4, 32, W), BF16),
        jax.ShapeDtypeStruct((W, W), F32),
    )

    def reduce_scratch(count):
        return [
            vmem((2, 16, count, 8, W), F32),
            vmem((16, count, 8, W), F32),
            vmem((16, count, 8, W), F32),
            vmem((15, count, 8, W), F32),
            vmem((8, count, 8, W), F32),
            vmem((16, count, 8, W), F32),
            vmem((2, 16, count, 8, W), F32),
        ]

    results = pl.pallas_call(
        body,
        out_shape=shapes,
        in_specs=[hbm] * 10,
        out_specs=(hbm,) * 5,
        scratch_shapes=[
            vmem((4, 4096, W), BF16),
            vmem((2, 4096, 128), F32),
            vmem((1024, 4096), BF16),
            vmem((2, 4, 4, 8, 2, 16, W), BF16),
            vmem((2, 4, 32, W), BF16),
            vmem((2, 4, 32, W), BF16),
            vmem((4, 8, 32, W), BF16),
            vmem((4, W, W), BF16),
            vmem((2, 4, 4, 2, 32, W), F32),
            vmem((2, 4, 4, 32, W), F32),
            vmem((2, 3, 4, 32, W), F32),
            vmem((W, W), F32),
            vmem((W, W), F32),
            vmem((BLK, BLK), F32),
            vmem((4, 32, W), BF16),
            vmem((4, 32, W), BF16),
            vmem((W, W), F32),
            vmem((W, W), BF16),
            vmem((W, W), F32),
            vmem((W, W), BF16),
            pltpu.SMEM((128,), jnp.int32),
            pltpu.SMEM((128,), jnp.int32),
            pltpu.SMEM((40,), F32),
            pltpu.SMEM((40,), jnp.int32),
        ]
        + reduce_scratch(2)
        + reduce_scratch(1)
        + [
            dma((13,)),
            dma((5,)),
            dma((8,)),
            dma((8,)),
            dma,
            dma((7,)),
            dma((7,)),
            dma((2, 3)),
            dma((2, 3)),
            dma((2, 4, 2, 2)),
            dma((2, 4, 2, 2)),
            dma((2, 8)),
            dma((2, 8)),
            dma((2, 8, 2)),
            dma((2, 8, 2)),
            dma((2, 8)),
            dma((2, 8)),
            dma((2, 4)),
            dma((2, 4)),
            dma((2, 3, 4)),
            dma((2, 3, 4)),
            dma((78,)),
            dma((78,)),
        ],
        compiler_params=pltpu.CompilerParams(
            collective_id=0, has_side_effects=True, vmem_limit_bytes=62 * 1024 * 1024
        ),
        name="selected_inversion",
    )(
        anc_inverse.reshape(4, 4096, W),
        first_lower.reshape(4, 32, W),
        second_lower.reshape(4, 32, W),
        second_top,
        struct_first,
        struct_keep,
        pivot_h,
        pivot_s,
        shifts,
        pole_index,
    )
    fc, fd, link, sc, sd = pl.pallas_call(
        hand_out,
        out_shape=shapes,
        in_specs=[hbm] * 5,
        out_specs=(hbm,) * 5,
        scratch_shapes=[vmem(s.shape, s.dtype) for s in shapes] + [dma((10,))],
        name="outputs",
    )(*results)
    return fc[:, None], fd, link, sc[:, None], sd


def solution(mesh):
    return jax.shard_map(
        per_device,
        mesh=mesh,
        in_specs=(
            P(None, "prow", None, None, "pcol", None),
            P(None, "prow", "pcol", None),
            P(None, "prow", "pcol", None),
            P(),
            P(),
            P(),
            P(),
            P(),
            P(),
            P(),
        ),
        out_specs=(P(None, "prow", "pcol", None), P(), P(), P(None, "prow", "pcol", None), P()),
        check_vma=False,
    )
```

time: 545 us -> 96.5 us (0.18)
  waiting for transfers between devices: 359 us -> 0 us
  other arithmetic: 120 us -> 0 us
  Pallas kernels: 0 us -> 95.8 us
  matrix products: 20.9 us -> 0 us
  local copies, waits for them, and re-layouts: 18.6 us -> 0 us
  between operations: 16.7 us -> 0.64 us
  starting transfers between devices: 8 us -> 0 us
    psum x2 -> x0, waiting for transfers between devices: 319 us -> none  [the longest x1 254 us: per_device(): lax.psum((first_term, cross_term, second_term), ('prow', 'pcol'))]
    another operation x19 -> x0, other arithmetic: 109 us -> none  [the longest x14 69.2 us: pivot_inverse(): factor = jnp.linalg.cholesky(h_block + shift * s_block)]
    pallas_call x0 -> x2, Pallas kernels: none -> 95.8 us  [the longest x1 93.8 us: per_device(): pl.pallas_call(body, out_shape=shapes, in_specs=[hbm] * 10, out_specs=(hb...]
    all_gather x1 -> x0, waiting for transfers between devices: 39.8 us -> none  [per_device(): gathered = lax.all_gather(stacked, 'prow', axis=1, tiled=True)]
    dot_general x7 -> x0, matrix products: 16.6 us -> none  [the longest x1 9.58 us: per_device(): jnp.einsum('axcy,cyz->xaz', inverse_rows, column_blocks, preferred_elemen...]
    another operation x19 -> x0, local copies, waits for them, and re-layouts: 8.04 us -> none  [the longest x15 7.99 us: pivot_inverse(): return jax.scipy.linalg.cho_solve((factor, True), identity)]
    all_to_all x1 -> x0, starting transfers between devices: 7.92 us -> none  [per_device(): lax.all_to_all(grouped, 'pcol', split_axis=2, concat_axis=3, tiled=True)]
  transfers between devices with their start and end apart: 4 -> 0, of which waited for: 3 -> 0; matrix products, arithmetic and copies ran while one was open for 24% -> 0% of each run, Pallas kernels for 0% -> 0%
where the time goes in v2:
time: 96.5 us; the launch traced here: 96.4 us
  Pallas kernels  95.8 us (99%)
    pallas_call x1, Pallas kernels, per_device(): pl.pallas_call(body, out_shape=shapes, in_specs=[hbm] * 10, out_specs=(hb...  93.8 us
    pallas_call x1, Pallas kernels, per_device(): pl.pallas_call(hand_out, out_shape=shapes, in_specs=[hbm] * 5, out_specs=...  1.95 us

profile of v2, /device:TPU:1, one launch (start us, length us, event | category | flops | bytes accessed | tf_op | source)
XLA Modules:
  0.0 96.4 jit_solution(9086981656578553247)
XLA Ops:
  0.6 93.8 %selected_inversion.1 = (bf16[4,32,256]{2,1,0:T(8,128)(2,1)}, f32[256,256]{1,0:T(8,128)}, bf16[256,256]{1,0:T(8,128)(2,1)}, bf16[4,32,256]{2,1,0:T(8,128)(2,1)}, f32[256,256]{1,0:T(8,128)}) custom-call(bf16[4,4096,256]{2,1,0:T(8,128)(2,1)} %bitcast.9, bf16[4,32,256]{2,1,0:T(8,128)(2,1)} %bitcast.10, bf16[4,32,256]{2,1,0:T(8,128)(2,1)} %bitcast.11, ...), custom_call_target="tpu_custom_call" | custom-call | tf_op jit(solution)/shard_map/selected_inversion/pallas_call | solution.py:650
  94.4 2.0 %outputs.1 = (bf16[4,32,256]{2,1,0:T(8,128)(2,1)}, f32[256,256]{1,0:T(8,128)}, bf16[256,256]{1,0:T(8,128)(2,1)}, bf16[4,32,256]{2,1,0:T(8,128)(2,1)}, f32[256,256]{1,0:T(8,128)}) custom-call(bf16[4,32,256]{2,1,0:T(8,128)(2,1)} %get-tuple-element.15.refs_0_, f32[256,256]{1,0:T(8,128)} %get-tuple-element.16.refs_1_, ...), custom_call_target="tpu_custom_call" | custom-call | tf_op jit(solution)/shard_map/outputs/pallas_call | solution.py:724

commit v3 on v2

--- a/solution.py
+++ b/solution.py
@@ -13,18 +13,23 @@
 W = 256
 BLK = 32
 LOW = 3
+FIRST = 10
 
 
 def gauss_jordan(x, first, last):
-    n = x.shape[0]
-    rows = lax.broadcasted_iota(jnp.int32, (n, n), 0)
-    cols = lax.broadcasted_iota(jnp.int32, (n, n), 1)
-    row1 = lax.broadcasted_iota(jnp.int32, (n, 1), 0)
-    col1 = lax.broadcasted_iota(jnp.int32, (1, n), 1)
+    n, lanes = x.shape
+    rows = lax.broadcasted_iota(jnp.int32, (n, lanes), 0)
+    cols = lax.broadcasted_iota(jnp.int32, (n, lanes), 1)
+    lane = lax.broadcasted_iota(jnp.int32, (1, lanes), 1)
+    ahead = [jnp.broadcast_to(x[:, k : k + 1], (n, lanes)) for k in range(first, last)]
     for k in range(first, last):
-        inv = 1.0 / x[k : k + 1, k : k + 1]
-        right = jnp.where(col1 == k, 1.0, x[k : k + 1, :]) * inv
-        left = jnp.where(row1 == k, 1.0, -x[:, k : k + 1])
+        col = ahead[k - first]
+        inv = 1.0 / col[k : k + 1, :]
+        left = jnp.where(rows == k, 1.0, -col)
+        for i in range(k + 1, last):
+            other = ahead[i - first]
+            ahead[i - first] = jnp.where(rows == k, 0.0, other) + left * (other[k : k + 1, :] * inv)
+        right = jnp.where(lane == k, 1.0, x[k : k + 1, :]) * inv
         x = jnp.where((rows == k) | (cols == k), 0.0, x) + left * right
     return x
 
@@ -68,6 +73,7 @@
     g,
     gs,
     gp,
+    dz,
     fc,
     sc,
     fd,
@@ -185,54 +191,17 @@
         lm[0, a] = (ll[0, a].astype(F32) * flag1[a]).astype(BF16)
         lm[1, a] = (ll[1, a].astype(F32) * flag2[a]).astype(BF16)
 
-    pl.semaphore_wait(barrier, 33)
-
-    def slice_of(zz):
-        return lm.at[:, zz // 2, pl.ds(pl.multiple_of(16 * (zz % 2), 16), 16)]
-
-    def spread(d):
-        zz = zr(d)
-        dst = m.at[:, zz // 2, x, q, zz % 2]
-        return remote(slice_of(zz), dst, sc_s.at[d], sc_r.at[q], dev(x, zz, z))
-
-    def keep_own():
-        return pltpu.make_async_copy(slice_of(z), m.at[:, z // 2, x, q, z % 2], sc_l)
-
-    @pl.when(q == z)
-    def _():
-        keep_own().start()
-
-    @pl.when(q != z)
-    def _():
-        spread(0).start()
-
-    for d in range(1, 8):
-        spread(d).start()
-
-    def relayout(a):
-        blocks[a].wait()
-
-        def widen(i, _):
-            rows = pl.ds(pl.multiple_of(i * 512, 512), 512)
-            for s in range(2):
-                a32[s, rows, :] = abuf[a, rows, s * 128 : (s + 1) * 128].astype(F32)
-            return 0
-
-        lax.fori_loop(0, 8, widen, 0)
-
-        def pick(c, _):
-            for s in range(2):
-                lanes = pl.ds(pl.multiple_of(c * W + s * 128, 128), 128)
-                abf[a * W : (a + 1) * W, lanes] = a32[s, pl.ds(c, W, stride=16), :].astype(BF16)
-            return 0
-
-        lax.fori_loop(0, 16, pick, 0)
-
     def inverse_pieces():
         for k in range(W // BLK):
             rows = pl.ds(k * BLK, BLK)
             for part in range(4):
-                block = g[rows, k * BLK : (k + 1) * BLK] if part == 0 else gp[...]
+                if part == 0:
+                    start = k * BLK // 128 * 128
+                    block = g[rows, start : start + 128]
+                    if k * BLK > start:
+                        block = pltpu.roll(block, 128 - (k * BLK - start), axis=1)
+                else:
+                    block = gp[...]
                 gp[...] = gauss_jordan(block, part * 8, part * 8 + 8)
                 yield
             panel = g[rows, :]
@@ -240,7 +209,7 @@
             unit = (lanes == lax.broadcasted_iota(jnp.int32, (BLK, W), 0) + k * BLK).astype(F32)
             inside = (lanes >= k * BLK) & (lanes < k * BLK + BLK)
             solved = jnp.dot(
-                gp[...], jnp.where(inside, -unit, panel), precision=HI, preferred_element_type=F32
+                gp[:, :BLK], jnp.where(inside, -unit, panel), precision=HI, preferred_element_type=F32
             )
             g[...] = g[...] - lax.dot_general(
                 panel, solved + unit, (((0,), (0,)), ((), ())), precision=HI, preferred_element_type=F32
@@ -254,10 +223,56 @@
         for _ in range(n):
             next(pieces, None)
 
-    relayout(0)
     for copy in pivots:
         copy.wait()
     g[...] = g[...] + shifts[pole[0]] * gs[...]
+    work(FIRST)
+    pl.semaphore_wait(barrier, 33)
+
+    def slice_of(h, zz):
+        return lm.at[h, zz // 2, pl.ds(pl.multiple_of(16 * (zz % 2), 16), 16)]
+
+    def spread(h, d):
+        zz = zr(d)
+        dst = m.at[h, zz // 2, x, q, zz % 2]
+        return remote(slice_of(h, zz), dst, sc_s.at[h, d], sc_r.at[h, q], dev(x, zz, z))
+
+    def keep_own(h):
+        return pltpu.make_async_copy(slice_of(h, z), m.at[h, z // 2, x, q, z % 2], sc_l.at[h])
+
+    def scatter(h):
+        @pl.when(q == z)
+        def _():
+            keep_own(h).start()
+
+        @pl.when(q != z)
+        def _():
+            spread(h, 0).start()
+
+        for d in range(1, 8):
+            spread(h, d).start()
+
+    scatter(0)
+    scatter(1)
+
+    def relayout(a):
+        blocks[a].wait()
+
+        def widen(i, _):
+            rows = pl.ds(pl.multiple_of(i * 512, 512), 512)
+            for s in range(2):
+                a32[s, rows, :] = abuf[a, rows, s * 128 : (s + 1) * 128].astype(F32)
+            return 0
+
+        lax.fori_loop(0, 8, widen, 0)
+
+        def pick(c, _):
+            for s in range(2):
+                lanes = pl.ds(pl.multiple_of(c * W + s * 128, 128), 128)
+                abf[a * W : (a + 1) * W, lanes] = a32[s, pl.ds(c, W, stride=16), :].astype(BF16)
+            return 0
+
+        lax.fori_loop(0, 16, pick, 0)
 
     lo, hi = pl.ds(0, LOW), pl.ds(LOW, 8 - LOW)
 
@@ -322,17 +337,17 @@
                 continue
             arrived(group(h, zr(-step * r), s), a2_s.at[h, r - 1, i, s], a2_r.at[h, r - 1, i, s])
 
-    def begin():
+    def begin(h):
         @pl.when(q == z)
         def _():
-            keep_own().wait()
+            keep_own(h).wait()
 
         @pl.when(q != z)
         def _():
-            arrived(m.at[:, z // 2, x, q, z % 2], sc_s.at[0], sc_r.at[q])
+            arrived(m.at[h, z // 2, x, q, z % 2], sc_s.at[h, 0], sc_r.at[h, q])
 
         for d in range(1, 8):
-            arrived(m.at[:, z // 2, x, qr(d), z % 2], sc_s.at[d], sc_r.at[qr(d)])
+            arrived(m.at[h, z // 2, x, qr(d), z % 2], sc_s.at[h, d], sc_r.at[h, qr(d)])
 
     def first_sends(h):
         for d in (1, 3, 2):
@@ -346,6 +361,27 @@
             arrived(m.at[h, z // 2, xr(-d), lo, z % 2], a1_s.at[h, d - 1], a1_r.at[h, d - 1])
         for s in range(2):
             low_z(h, 1, s)
+            if h == 0:
+                jump(h, 0, 2, s)
+
+    def jump(h, origin, r, s):
+        for i, step in enumerate((1, -1)):
+            if r == 4 and s != i:
+                continue
+            ref = group(h, zr(-step * origin), s)
+            target = dev(x, zr(step * (r - origin)), q)
+            send(ref, ref, a2_s.at[h, r - 1, i, s], a2_r.at[h, r - 1, i, s], target)
+
+    def low_far(h):
+        for s in range(2):
+            low_z_wait(h, 2, s)
+            jump(h, 2, 3, s)
+            jump(h, 2, 4, s)
+
+    def low_rest(h):
+        for r in (1, 3, 4):
+            for s in range(2):
+                low_z_wait(h, r, s)
 
     def low(h, r):
         for s in range(2):
@@ -456,7 +492,17 @@
         xx, yy = (x + dx) % NX, (y + dy) % NY
         return xx * NY + yy, dev(xx, z, yy * 2 + core)
 
-    def all_reduce(base, t, w0, u, w1, w3, w4, wf):
+    half = pl.ds(pl.multiple_of((1 - core) * 128, 128), 128)
+
+    def swap_inverse():
+        send(g.at[half], dz, p_s.at[78], p_r.at[78], dev(x, z, q + 1 - 2 * core))
+
+    def inverse_rows(k):
+        own = g[pl.ds(pl.multiple_of((core * 16 + spot) * 8, 8), 8), :]
+        other = dz[pl.ds(pl.multiple_of(spot * 8, 8), 8), :]
+        return jnp.where(z == 0, jnp.where(core == k, own, other), 0.0)
+
+    def all_reduce(base, t, w0, u, w1, w3, w4, wf, enter):
         def sems(i):
             return p_s.at[base + i], p_r.at[base + i]
 
@@ -473,7 +519,7 @@
         for i in range(15):
             arrived(w1.at[i], *sems(1 + i))
             total = total + w1[i]
-        w3[z] = total
+        enter(w3, total)
         for d in range(1, 8):
             send(w3.at[z], w3.at[z], *sems(15 + d), dev(x, zr(d), q))
         yield
@@ -494,52 +540,62 @@
         arrived(wf.at[1 - core], *sems(38))
         yield
 
-    reduce_a = all_reduce(0, ta, wa0, ua, wa1, wa3, wa4, waf)
-    reduce_b = all_reduce(39, tb, wb0, ub, wb1, wb3, wb4, wbf)
-
+    def enter_a(w3, total):
+        w3[z, 0] = total[0] + inverse_rows(0)
+        w3[z, 1] = total[1]
+
+    def enter_b(w3, total):
+        w3[z, 0] = total[0] - inverse_rows(1)
+
+    reduce_a = all_reduce(0, ta, wa0, ua, wa1, wa3, wa4, waf, enter_a)
+    reduce_b = all_reduce(39, tb, wb0, ub, wb1, wb3, wb4, wbf, enter_b)
+
+    relayout(0)
     relayout(1)
-    relayout(2)
-    begin()
+    work(5)
+    begin(0)
     first_sends(0)
     share_rows()
+    relayout(2)
+    begin(1)
+    work(2)
+    low_start(0)
+    high_second(0)
+    work(4)
+    first_sends(1)
     relayout(3)
-    work(1)
-    low_start(0)
-    work(1)
-    high_second(0)
     work(3)
-    low(0, 1)
+    low_far(0)
     high_third(0)
-    first_sends(1)
     hop(0, 0, 1, -1, 2, -2)
-    work(3)
-    low(0, 2)
     low_start(1)
     high_second(1)
+    work(4)
     hop(0, 3, -3, 4)
-    work(4)
-    low(0, 3)
-    work(2)
+    low_rest(0)
+    hop_wait(0)
+    multiply(0)
     low(1, 1)
     high_third(1)
-    work(2)
-    low(0, 4)
-    hop_wait(0)
-    multiply(0)
+    pair_sum(0)
     hop(1, 0, 1, -1, 2, -2)
+    work(8)
     low(1, 2)
-    pair_sum(0)
     hop(1, 3, -3, 4)
-    work(6)
+    work(8)
+    turn_rows()
     low(1, 3)
-    turn_rows()
-    work(6)
+    work(8)
+    tops.wait()
+    finish_first()
+    first = fc[...].reshape(128, W)
+    ta[:, :, 0] = contract(lm[0].reshape(128, W), first).reshape(2, 16, 8, W)
+    ta[:, :, 1] = contract(first, lm[1].reshape(128, W)).reshape(2, 16, 8, W)
+    next(reduce_a)
     low(1, 4)
+    next(reduce_a)
     hop_wait(1)
     multiply(1)
-
-    owner1 = ((prow == 0) & (q == 0)).astype(F32)
-    owner2 = ((prow == 0) & (q == 1)).astype(F32)
 
     def second_term():
         total = jnp.zeros((W, W), F32)
@@ -548,25 +604,20 @@
                 total = total + jnp.dot(mbt[a], piece, preferred_element_type=F32)
         return total
 
+    tb[...] = second_term().reshape(2, 16, 1, 8, W)
+    next(reduce_b)
+    work(1)
+    next(reduce_b)
     work(40)
-    tb[...] = (second_term() - owner2 * g[...]).reshape(2, 16, 1, 8, W)
-    next(reduce_b)
-    tops.wait()
-    finish_first()
-    first = fc[...].reshape(128, W)
-    ta[:, :, 0] = (contract(lm[0].reshape(128, W), first) + owner1 * g[...]).reshape(2, 16, 8, W)
-    ta[:, :, 1] = contract(first, lm[1].reshape(128, W)).reshape(2, 16, 8, W)
+    swap_inverse()
+    pair_sum(1)
+    arrived(dz, p_s.at[78], p_r.at[78])
     next(reduce_a)
-    next(reduce_b)
-    next(reduce_a)
-    pair_sum(1)
     next(reduce_b)
     next(reduce_a)
     next(reduce_b)
     next(reduce_a)
     finish_second()
-    next(reduce_b)
-    next(reduce_a)
     next(reduce_a)
     first_diag = -waf[:, :, 0].reshape(W, W)
     fd[...] = first_diag
@@ -579,19 +630,21 @@
     for piece in split(cross_sum):
         tail = tail + contract(piece, top[...])
     next(reduce_b)
+    next(reduce_b)
     sd[...] = wbf[:, :, 0].reshape(W, W) + tail
     put(sd, sd_out, 4)
 
     for copy in sent:
         copy.wait_send()
 
-    @pl.when(q != z)
-    def _():
-        spread(0).wait_send()
-
-    for d in range(1, 8):
-        spread(d).wait_send()
     for h in range(2):
+
+        @pl.when(q != z)
+        def _(h=h):
+            spread(h, 0).wait_send()
+
+        for d in range(1, 8):
+            spread(h, d).wait_send()
         for a in range(4):
             pair_copy(h, a).wait_send()
             for d in (1, 2, 3):
@@ -666,7 +719,8 @@
             vmem((2, 3, 4, 32, W), F32),
             vmem((W, W), F32),
             vmem((W, W), F32),
-            vmem((BLK, BLK), F32),
+            vmem((BLK, 128), F32),
+            vmem((128, W), F32),
             vmem((4, 32, W), BF16),
             vmem((4, 32, W), BF16),
             vmem((W, W), F32),
@@ -683,9 +737,9 @@
         + [
             dma((13,)),
             dma((5,)),
-            dma((8,)),
-            dma((8,)),
-            dma,
+            dma((2, 8)),
+            dma((2, 8)),
+            dma((2,)),
             dma((7,)),
             dma((7,)),
             dma((2, 3)),
@@ -702,8 +756,8 @@
             dma((2, 4)),
             dma((2, 3, 4)),
             dma((2, 3, 4)),
-            dma((78,)),
-            dma((78,)),
+            dma((79,)),
+            dma((79,)),
         ],
         compiler_params=pltpu.CompilerParams(
             collective_id=0, has_side_effects=True, vmem_limit_bytes=62 * 1024 * 1024

time: 96.5 us -> 86.2 us (0.89)
  Pallas kernels: 95.8 us -> 85.3 us
    pallas_call x1, Pallas kernels: 93.8 us -> 83.3 us  [per_device(): pl.pallas_call(body, out_shape=shapes, in_specs=[hbm] * 10, out_specs=(hb...]
where the time goes in v3:
time: 86.2 us; the launch traced here: 86.1 us
  Pallas kernels  85.3 us (99%)
    pallas_call x1, Pallas kernels, per_device(): pl.pallas_call(body, out_shape=shapes, in_specs=[hbm] * 10, out_specs=(hb...  83.3 us
    pallas_call x1, Pallas kernels, per_device(): pl.pallas_call(hand_out, out_shape=shapes, in_specs=[hbm] * 5, out_specs=...  1.95 us

profile of v3, /device:TPU:1, one launch (start us, length us, event | category | flops | bytes accessed | tf_op | source)
XLA Modules:
  0.0 86.1 jit_solution(16215149160249434828)
XLA Ops:
  0.6 83.3 %selected_inversion.1 = (bf16[4,32,256]{2,1,0:T(8,128)(2,1)}, f32[256,256]{1,0:T(8,128)}, bf16[256,256]{1,0:T(8,128)(2,1)}, bf16[4,32,256]{2,1,0:T(8,128)(2,1)}, f32[256,256]{1,0:T(8,128)}) custom-call(bf16[4,4096,256]{2,1,0:T(8,128)(2,1)} %bitcast.9, bf16[4,32,256]{2,1,0:T(8,128)(2,1)} %bitcast.10, bf16[4,32,256]{2,1,0:T(8,128)(2,1)} %bitcast.11, ...), custom_call_target="tpu_custom_call" | custom-call | tf_op jit(solution)/shard_map/selected_inversion/pallas_call | solution.py:703
  84.0 2.0 %outputs.1 = (bf16[4,32,256]{2,1,0:T(8,128)(2,1)}, f32[256,256]{1,0:T(8,128)}, bf16[256,256]{1,0:T(8,128)(2,1)}, bf16[4,32,256]{2,1,0:T(8,128)(2,1)}, f32[256,256]{1,0:T(8,128)}) custom-call(bf16[4,32,256]{2,1,0:T(8,128)(2,1)} %get-tuple-element.15.refs_0_, f32[256,256]{1,0:T(8,128)} %get-tuple-element.16.refs_1_, ...), custom_call_target="tpu_custom_call" | custom-call | tf_op jit(solution)/shard_map/outputs/pallas_call | solution.py:778

commit v4 on v3

--- a/solution.py
+++ b/solution.py
@@ -361,8 +361,6 @@
             arrived(m.at[h, z // 2, xr(-d), lo, z % 2], a1_s.at[h, d - 1], a1_r.at[h, d - 1])
         for s in range(2):
             low_z(h, 1, s)
-            if h == 0:
-                jump(h, 0, 2, s)
 
     def jump(h, origin, r, s):
         for i, step in enumerate((1, -1)):
@@ -432,6 +430,30 @@
                 abf[pl.ds(pl.multiple_of(a * W, W), W), :], weights, preferred_element_type=F32
             )
             prod[h, a] = part.reshape(4, 2, 32, W)
+            pair_copy(h, a).start()
+            return 0
+
+        lax.fori_loop(0, 4, rows, 0)
+
+    last = ((z + 4) % NZ) // 2
+
+    def part_product(a, k, h):
+        left = abf[pl.ds(pl.multiple_of(a * W, W), W), pl.ds(pl.multiple_of(k * 1024, 1024), 1024)]
+        return jnp.dot(left, m[h, k].reshape(4 * W, W), preferred_element_type=F32)
+
+    def multiply_early(h):
+        def rows(a, _):
+            total = part_product(a, (last + 1) % 4, h)
+            for d in (2, 3):
+                total = total + part_product(a, (last + d) % 4, h)
+            prod[h, a] = total.reshape(4, 2, 32, W)
+            return 0
+
+        lax.fori_loop(0, 4, rows, 0)
+
+    def multiply_last(h):
+        def rows(a, _):
+            prod[h, a] = prod[h, a] + part_product(a, last, h).reshape(4, 2, 32, W)
             pair_copy(h, a).start()
             return 0
 
@@ -565,16 +587,19 @@
     first_sends(1)
     relayout(3)
     work(3)
-    low_far(0)
+    low(0, 1)
     high_third(0)
     hop(0, 0, 1, -1, 2, -2)
     low_start(1)
     high_second(1)
     work(4)
     hop(0, 3, -3, 4)
-    low_rest(0)
+    low(0, 2)
+    low(0, 3)
     hop_wait(0)
-    multiply(0)
+    multiply_early(0)
+    low(0, 4)
+    multiply_last(0)
     low(1, 1)
     high_third(1)
     pair_sum(0)
@@ -592,10 +617,11 @@
     ta[:, :, 0] = contract(lm[0].reshape(128, W), first).reshape(2, 16, 8, W)
     ta[:, :, 1] = contract(first, lm[1].reshape(128, W)).reshape(2, 16, 8, W)
     next(reduce_a)
+    hop_wait(1)
+    next(reduce_a)
+    multiply_early(1)
     low(1, 4)
-    next(reduce_a)
-    hop_wait(1)
-    multiply(1)
+    multiply_last(1)
 
     def second_term():
         total = jnp.zeros((W, W), F32)

time: 86.2 us -> 84.6 us (0.981)
  Pallas kernels: 85.3 us -> 83.7 us
    pallas_call x1, Pallas kernels: 83.3 us -> 81.8 us  [per_device(): pl.pallas_call(body, out_shape=shapes, in_specs=[hbm] * 10, out_specs=(hb...]
where the time goes in v4:
time: 84.6 us; the launch traced here: 84.5 us
  Pallas kernels  83.7 us (99%)
    pallas_call x1, Pallas kernels, per_device(): pl.pallas_call(body, out_shape=shapes, in_specs=[hbm] * 10, out_specs=(hb...  81.8 us
    pallas_call x1, Pallas kernels, per_device(): pl.pallas_call(hand_out, out_shape=shapes, in_specs=[hbm] * 5, out_specs=...  1.95 us

profile of v4, /device:TPU:1, one launch (start us, length us, event | category | flops | bytes accessed | tf_op | source)
XLA Modules:
  0.0 84.5 jit_solution(12126521286475877997)
XLA Ops:
  0.6 81.8 %selected_inversion.1 = (bf16[4,32,256]{2,1,0:T(8,128)(2,1)}, f32[256,256]{1,0:T(8,128)}, bf16[256,256]{1,0:T(8,128)(2,1)}, bf16[4,32,256]{2,1,0:T(8,128)(2,1)}, f32[256,256]{1,0:T(8,128)}) custom-call(bf16[4,4096,256]{2,1,0:T(8,128)(2,1)} %bitcast.9, bf16[4,32,256]{2,1,0:T(8,128)(2,1)} %bitcast.10, bf16[4,32,256]{2,1,0:T(8,128)(2,1)} %bitcast.11, ...), custom_call_target="tpu_custom_call" | custom-call | tf_op jit(solution)/shard_map/selected_inversion/pallas_call | solution.py:729
  82.4 2.0 %outputs.1 = (bf16[4,32,256]{2,1,0:T(8,128)(2,1)}, f32[256,256]{1,0:T(8,128)}, bf16[256,256]{1,0:T(8,128)(2,1)}, bf16[4,32,256]{2,1,0:T(8,128)(2,1)}, f32[256,256]{1,0:T(8,128)}) custom-call(bf16[4,32,256]{2,1,0:T(8,128)(2,1)} %get-tuple-element.15.refs_0_, f32[256,256]{1,0:T(8,128)} %get-tuple-element.16.refs_1_, ...), custom_call_target="tpu_custom_call" | custom-call | tf_op jit(solution)/shard_map/outputs/pallas_call | solution.py:804
